TPU v7x, 32 devices: a whole 2x2x4 slice. The times are simulated.
32 devices in a mesh: elem: 16 (over z, x, core), head: 2 (over y).
Axes of the slice: x: 2, y: 2, z: 4, core: 2. Of those that a mesh axis runs over, the one named last changes fastest.
Arguments:
- features: bfloat16 [16384, 512], P('elem'), may hold values from -6 to 6
- out_grad: bfloat16 [16384, 512], P('elem'), may hold values from -6 to 6
- bin_order: int32 [16384], P('elem'), may hold values from 0 to 16383, as said below
- key_lists: int32 [128, 12], P('elem'), may hold values from 0 to 127, as said below
- list_counts: int32 [128], P('elem'), may hold values from 1 to 12, as said below
- attn_gain: float32 [512], replicated, may hold values from 0.1 to 1.9
- query_weight: bfloat16 [512, 512], P(None, 'head')
- key_weight: bfloat16 [512, 512], P(None, 'head')
- value_weight: bfloat16 [512, 512], P(None, 'head'), may hold values from -0.25 to 0.25
- out_weight: bfloat16 [512, 512], P('head'), may hold values from -0.25 to 0.25
- ffn_gain: float32 [512], replicated, may hold values from 0.1 to 1.9
- ffn_in: bfloat16 [512, 2048], P(None, 'head'), may hold values from -0.25 to 0.25
- ffn_out: bfloat16 [2048, 512], P('head'), may hold values from -0.125 to 0.125
Outputs:
- output: bfloat16 [16384, 512], P('elem', 'head')
- input_grad: float32 [16384, 512], P('elem', 'head')
Inputs may be any that keep to these rules, and one draw needn't show every extreme that they name: `bin_order`: the rows of region e, numbers e * 1024 to (e + 1) * 1024 - 1, hold a permutation of those same numbers. `key_lists`: slot 0 of row b is b; the other slots hold distinct blocks other than b, all of the regions r - 1, r and r + 1 modulo 16, where r = b // 8 and region r holds blocks r * 8 to (r + 1) * 8 - 1; in row r * 8 of every region, slot 1 is a block of region r - 1 and slot 2 a block of region r + 1. list_counts[r * 8] = 12 for every region r.
All inputs are finite; a program needn't handle non-finite values.
Results may differ from a plain program's by a relative error of at most 0.024.
Values may be sent and summed in bfloat16 or wider, within the bound.
No kernel may reach another device: no remote copies, remote signals or barrier semaphores. Data moves between devices by JAX's collectives and lax.ppermute only.
A program may use at most 128 MiB of HBM per device.

v0:
```python
import jax
import jax.numpy as jnp
from jax import lax
from jax.sharding import PartitionSpec as P

HD = 64


EPSILON = 1e-05


def padded(block, sides, width):
    for axis, dim in sides:
        count = lax.axis_size(axis)
        forward = [(i, i + 1) for i in range(count - 1)]
        forward.append((count - 1, 0))
        backward = [(target, source) for source, target in forward]
        low = lax.ppermute(
            lax.slice_in_dim(block, block.shape[dim] - width, None, axis=dim), axis, forward
        )
        high = lax.ppermute(lax.slice_in_dim(block, 0, width, axis=dim), axis, backward)
        block = jnp.concatenate([low, block, high], axis=dim)
    return block


def from_behind(value, axis, steps):
    count = lax.axis_size(axis)
    pairs = [(source, (source + steps) % count) for source in range(count)]
    return lax.ppermute(value, axis, pairs)


def row_scale(values):
    return lax.rsqrt(jnp.mean(values * values, axis=-1, keepdims=True) + EPSILON)


def local(
    features,
    out_grad,
    bin_order,
    key_lists,
    list_counts,
    attn_gain,
    query_weight,
    key_weight,
    value_weight,
    out_weight,
    ffn_gain,
    ffn_in,
    ffn_out,
):
    row_count, model_width = features.shape
    block_count = key_lists.shape[0]
    block_len = row_count // block_count
    col_share = query_weight.shape[1]
    local_heads = col_share // HD
    scale_for_scores = HD ** (-0.5)
    highest_precision = lax.Precision.HIGHEST
    region = lax.axis_index("elem")
    regions = lax.axis_size("elem")
    head_group = lax.axis_index("head")
    col_start = head_group * col_share
    positions = bin_order - region * row_count
    owners = key_lists // block_count
    relative = jnp.mod(owners - region + 1, regions)
    buffer_index = relative * block_count + key_lists % block_count
    top_count = jnp.max(list_counts)
    wide_blocks = 3 * block_count
    block_ids = jnp.arange(wide_blocks, dtype=jnp.int32)
    ordered_rows = jnp.take(features, positions, axis=0).astype(jnp.float32)
    first_scale = row_scale(ordered_rows)
    first_norm = ordered_rows * first_scale
    normed = (first_norm * attn_gain).astype(jnp.bfloat16)
    queries = jnp.dot(normed, query_weight, preferred_element_type=jnp.float32).astype(jnp.bfloat16)
    pair_weights = jnp.concatenate([key_weight, value_weight], axis=1)
    widened = padded(normed, (("elem", 0),), row_count)
    pair_rows = jnp.dot(widened, pair_weights, preferred_element_type=jnp.float32).astype(
        jnp.bfloat16
    )
    wide_rows = 3 * row_count
    pair_blocks = pair_rows.reshape(wide_blocks, block_len, 2 * col_share)
    query_blocks = queries.reshape(block_count, block_len, local_heads, HD)

    def slot_table(slot_pos):
        picked = lax.dynamic_index_in_dim(buffer_index, slot_pos, axis=1, keepdims=False)
        return picked[:, None] == block_ids[None, :]

    def slot_scores(slot_pos):
        table = slot_table(slot_pos)
        tiles = jnp.einsum(
            "bc,ckf->bkf",
            table.astype(jnp.bfloat16),
            pair_blocks,
            preferred_element_type=jnp.float32,
        ).astype(jnp.bfloat16)
        key_tile_blocks = tiles[:, :, :col_share].reshape(block_count, block_len, local_heads, HD)
        value_tile_blocks = tiles[:, :, col_share:].reshape(block_count, block_len, local_heads, HD)
        attention_scores = (
            jnp.einsum(
                "bqhd,bkhd->bhqk", query_blocks, key_tile_blocks, preferred_element_type=jnp.float32
            )
            * scale_for_scores
        )
        live_mask = (slot_pos < list_counts)[:, None, None, None]
        return (
            jnp.where(live_mask, attention_scores, -jnp.inf),
            table,
            key_tile_blocks,
            value_tile_blocks,
        )

    first_scores, first_table, first_keys, first_values = slot_scores(0)
    run_max = jnp.max(first_scores, axis=-1)
    run_total = jnp.sum(jnp.exp(first_scores - run_max[..., None]), axis=-1)

    def stats_step(slot_pos, carried):
        old_max, old_total = carried
        attention_scores, table, key_tile_blocks, value_tile_blocks = slot_scores(slot_pos)
        new_max = jnp.maximum(old_max, jnp.max(attention_scores, axis=-1))
        new_total = old_total * jnp.exp(old_max - new_max) + jnp.sum(
            jnp.exp(attention_scores - new_max[..., None]), axis=-1
        )
        return (new_max, new_total)

    run_max, run_total = lax.fori_loop(1, top_count, stats_step, (run_max, run_total))
    log_total = run_max + jnp.log(run_total)

    def output_step(slot_pos, running):
        attention_scores, table, key_tile_blocks, value_tile_blocks = slot_scores(slot_pos)
        attn_probs = jnp.exp(attention_scores - log_total[..., None]).astype(jnp.bfloat16)
        return running + jnp.einsum(
            "bhqk,bkhd->bqhd", attn_probs, value_tile_blocks, preferred_element_type=jnp.float32
        )

    attended_sum = lax.fori_loop(
        0, top_count, output_step, jnp.zeros((block_count, block_len, local_heads, HD), jnp.float32)
    )
    attended_output = attended_sum.reshape(row_count, col_share).astype(jnp.bfloat16)
    mixed_heads = lax.psum(
        jnp.dot(attended_output, out_weight, preferred_element_type=jnp.float32).astype(
            jnp.bfloat16
        ),
        "head",
    ).astype(jnp.float32)
    hidden_in = ordered_rows + mixed_heads
    second_scale = row_scale(hidden_in)
    second_norm = hidden_in * second_scale
    normed_two = (second_norm * ffn_gain).astype(jnp.bfloat16)
    pre_act = jnp.dot(normed_two, ffn_in, preferred_element_type=jnp.float32)
    activated = jax.nn.gelu(pre_act).astype(jnp.bfloat16)
    ffn_terms = jnp.dot(activated, ffn_out, preferred_element_type=jnp.float32)
    ffn_total = lax.psum(ffn_terms.astype(jnp.bfloat16), "head").astype(jnp.float32)
    out_sorted = lax.dynamic_slice_in_dim(hidden_in + ffn_total, col_start, col_share, 1).astype(
        jnp.bfloat16
    )
    grad_sorted = jnp.take(out_grad, positions, axis=0)
    grad_act = jnp.dot(grad_sorted, ffn_out.T, preferred_element_type=jnp.float32)
    gelu_value, gelu_pull = jax.vjp(jax.nn.gelu, pre_act)
    grad_pre = gelu_pull(grad_act)[0].astype(jnp.bfloat16)
    norm_grad = lax.psum(
        jnp.dot(grad_pre, ffn_in.T, preferred_element_type=jnp.float32).astype(jnp.bfloat16), "head"
    ).astype(jnp.float32)
    scaled_grad = norm_grad * ffn_gain
    grad_hidden = grad_sorted.astype(jnp.float32) + second_scale * (
        scaled_grad - second_norm * jnp.mean(scaled_grad * second_norm, axis=-1, keepdims=True)
    )
    grad_mixed = jnp.dot(
        grad_hidden.astype(jnp.bfloat16), out_weight.T, preferred_element_type=jnp.float32
    ).astype(jnp.bfloat16)
    output = jnp.zeros_like(out_sorted).at[positions].set(out_sorted)
    grad_blocks = grad_mixed.reshape(block_count, block_len, local_heads, HD)
    attended_blocks = attended_output.reshape(block_count, block_len, local_heads, HD)
    deltas = jnp.einsum(
        "bqhd,bqhd->bhq", grad_blocks, attended_blocks, preferred_element_type=jnp.float32
    )

    def back_step(slot_pos, carried):
        query_gradient, grad_pair_blocks = carried
        attention_scores, table, key_tile_blocks, value_tile_blocks = slot_scores(slot_pos)
        complete_probabilities = jnp.exp(attention_scores - log_total[..., None])
        probability_gradient = jnp.einsum(
            "bqhd,bkhd->bhqk", grad_blocks, value_tile_blocks, preferred_element_type=jnp.float32
        )
        score_gradient = (
            complete_probabilities * (probability_gradient - deltas[..., None])
        ).astype(jnp.bfloat16)
        query_gradient = (
            query_gradient
            + jnp.einsum(
                "bhqk,bkhd->bqhd",
                score_gradient,
                key_tile_blocks,
                preferred_element_type=jnp.float32,
            )
            * scale_for_scores
        )
        key_portion = (
            jnp.einsum(
                "bhqk,bqhd->bkhd", score_gradient, query_blocks, preferred_element_type=jnp.float32
            )
            * scale_for_scores
        )
        value_portion = jnp.einsum(
            "bhqk,bqhd->bkhd",
            complete_probabilities.astype(jnp.bfloat16),
            grad_blocks,
            preferred_element_type=jnp.float32,
        )
        portion = jnp.concatenate(
            [
                key_portion.reshape(block_count, block_len, col_share),
                value_portion.reshape(block_count, block_len, col_share),
            ],
            axis=2,
        )
        grad_pair_blocks = grad_pair_blocks + jnp.einsum(
            "bc,bkf->ckf", table.astype(jnp.float32), portion, precision=highest_precision
        )
        return (query_gradient, grad_pair_blocks)

    zero_query = jnp.zeros((block_count, block_len, local_heads, HD), jnp.float32)
    zero_wide = jnp.zeros((wide_blocks, block_len, 2 * col_share), jnp.float32)
    query_gradient, grad_pair_blocks = lax.fori_loop(
        0, top_count, back_step, (zero_query, zero_wide)
    )
    grad_pairs = grad_pair_blocks.reshape(wide_rows, 2 * col_share)
    pair_wide = pair_weights.astype(jnp.float32)
    query_part = jnp.dot(
        query_gradient.reshape(row_count, col_share),
        query_weight.astype(jnp.float32).T,
        precision=highest_precision,
    )
    grad_wide = jnp.dot(grad_pairs, pair_wide.T, precision=highest_precision)
    from_right = from_behind(grad_wide[:row_count].astype(jnp.bfloat16), "elem", -1).astype(
        jnp.float32
    )
    from_left = from_behind(grad_wide[2 * row_count :].astype(jnp.bfloat16), "elem", 1).astype(
        jnp.float32
    )
    group_term = query_part + grad_wide[row_count : 2 * row_count] + from_right + from_left
    grad_norm = lax.psum(group_term.astype(jnp.bfloat16), "head").astype(jnp.float32)
    scaled_one = grad_norm * attn_gain
    row_gradients = grad_hidden + first_scale * (
        scaled_one - first_norm * jnp.mean(scaled_one * first_norm, axis=-1, keepdims=True)
    )
    grad_share = lax.dynamic_slice_in_dim(row_gradients, col_start, col_share, 1)
    input_grad = jnp.zeros_like(grad_share).at[positions].set(grad_share)
    return (output, input_grad)


def solution(mesh):
    in_specs = (
        P("elem", None),
        P("elem", None),
        P("elem"),
        P("elem", None),
        P("elem"),
        P(),
        P(None, "head"),
        P(None, "head"),
        P(None, "head"),
        P("head", None),
        P(),
        P(None, "head"),
        P("head", None),
    )
    out_specs = (P("elem", "head"), P("elem", "head"))
    return jax.shard_map(local, mesh=mesh, in_specs=in_specs, out_specs=out_specs, check_vma=False)
```

profile of v0, /device:TPU:0, one launch (start us, length us, event | category | flops | bytes accessed | tf_op | source)
XLA Modules:
  0.0 722.3 jit_solution(11235072406354910245)
XLA Ops:
  8.6 5.4 gather_fusion
  15.2 5.4 collective-permute-start.1
  28.5 4.4 collective-permute-done.1
  32.9 4.8 collective-permute-done
  37.7 3.3 convolution_convert_fusion.2
  41.1 3.5 copy.52
  48.6 56.3 %while.37 = (s32[]{:T(128)}, f32[8,4,128]{2,1,0:T(4,128)S(1)}, f32[8,4,128]{2,1,0:T(4,128)S(1)}, s32[]{:T(128)}, s32[8]{0:T(128)S(1)}, /*index=5*/s32[8,12]{0,1:...) while((s32[]{:T(128)}, f32[8,4,128]{2,1,0:T(4,128)S(1)}, ...), condition=%wide.region_7.9_spmd.clone, body=%wide.region_4.8_spmd.clone.sunk | while | flops 95953104 | bytes 11747639 | solution.py:124
  106.1 95.0 %while.38 = (s32[]{:T(128)}, f32[8,128,4,64]{1,3,2,0:T(8,128)}, s32[]{:T(128)}, s32[8,12]{0,1:T(8,128)S(1)}, bf16[24,128,512]{2,0,1:T(8,128)(2,1)}, /*index=5*/s...) while((s32[]{:T(128)}, f32[8,128,4,64]{1,3,2,0:T(8,128)}, ...), condition=%wide.region_9.11_spmd.clone, body=%wide.region_8.10_spmd.clone.sunk | while | flops 162267344 | bytes 12075311 | solution.py:134
  110.3 3.7 fusion.180
  118.1 3.7 fusion.180
  126.0 3.7 fusion.180
  133.9 3.7 fusion.180
  141.7 3.7 fusion.180
  149.6 3.7 fusion.180
  157.4 3.7 fusion.180
  165.3 3.7 fusion.180
  173.2 3.7 fusion.180
  181.0 3.7 fusion.180
  188.9 3.7 fusion.180
  196.8 3.7 fusion.180
  204.4 5.1 gather_fusion.1
  209.4 40.8 %all-reduce.5.cloned.1.call-done = bf16[1024,512]{1,0:T(8,128)(2,1)} async-done(((bf16[1024,512]{1,0:T(8,128)(2,1)}), bf16[1024,512]{1,0:T(8,128)(2,1)}) %all-reduce.5.cloned.1.call-update) | async-done | bytes 1048592 | tf_op jit(solution)/shard_map/psum | solution.py:138
  252.5 3.4 fusion.60
  255.8 7.6 %fusion.58 = bf16[1024,512]{1,0:T(8,128)(2,1)} fusion(bf16[512,1024]{1,0:T(8,128)(2,1)S(1)} %copy-done, f32[1024,1024]{1,0:T(8,128)} %fusion.60, bf16[1024,512]{1,0:T(8,128)(2,1)} %param.33, bf16[1024,512]{1,0:T(8,128)(2,1)} %gather_fusion.1, pred[1024]{0:T(1024)(128)(4,1)S(1)} %get-tuple-element.344), kind=kOutput, calls=%fused_computation.94 | convolution fusion | flops 2169503744 | bytes 8389632 | tf_op jit(solution)/shard_map/dot_general | solution.py:160
  263.7 40.0 %all-reduce.7.cloned.1.call-done = bf16[1024,512]{1,0:T(8,128)(2,1)} async-done(((bf16[1024,512]{1,0:T(8,128)(2,1)}), bf16[1024,512]{1,0:T(8,128)(2,1)}) %all-reduce.7.cloned.1.call-update) | async-done | bytes 1048592 | tf_op jit(solution)/shard_map/psum | solution.py:159
  311.3 3.5 broadcast_in_dim.92
  314.8 279.2 %while.39 = (s32[]{:T(128)}, f32[8,128,4,64]{1,3,2,0:T(8,128)}, f32[24,128,512]{2,0,1:T(8,128)}, s32[]{:T(128)}, s32[8,12]{0,1:T(8,128)S(1)}, /*index=5*/bf16[24...) while((s32[]{:T(128)}, f32[8,128,4,64]{1,3,2,0:T(8,128)}, ...), condition=%wide.region_17.19_spmd.clone, body=%wide.region_16.18_spmd.clone.sunk | while | flops 518783360 | bytes 61374988 | solution.py:222
  331.3 6.7 convolution_add_fusion.2
  354.5 6.7 convolution_add_fusion.2
  377.7 6.7 convolution_add_fusion.2
  400.9 6.7 convolution_add_fusion.2
  424.1 6.7 convolution_add_fusion.2
  447.3 6.7 convolution_add_fusion.2
  470.5 6.7 convolution_add_fusion.2
  493.7 6.7 convolution_add_fusion.2
  516.9 6.7 convolution_add_fusion.2
  540.1 6.7 convolution_add_fusion.2
  563.3 6.7 convolution_add_fusion.2
  586.5 6.7 convolution_add_fusion.2
  594.0 6.5 copy.60
  600.5 5.5 fusion.108
  606.3 4.7 collective-permute-start.2
  614.0 9.3 %collective-permute-done.3 = bf16[1024,512]{1,0:T(8,128)(2,1)S(1)} collective-permute-done((bf16[1024,512]{1,0:T(8,128)(2,1)S(1)}, bf16[1024,512]{1,0:T(8,128)(2,1)S(1)}, u32[]{:S(2)}, u32[]{:S(2)}) %collective-permute-start.3) | collective-permute-done | bytes 1048608 | tf_op jit(solution)/shard_map/ppermute | solution.py:29
  623.3 3.0 fusion.54
  626.4 71.7 %all-reduce.9.cloned.1.call-done = (bf16[1024,512]{1,0:T(8,128)(2,1)}, bf16[1024,512]{1,0:T(8,128)(2,1)}) async-done(((bf16[1024,512]{1,0:T(8,128)(2,1)}, bf16[1024,512]{1,0:T(8,128)(2,1)}), (bf16[1024,512]{1,0:T(8,128)(2,1)}, bf16[1024,512]{1,0:T(8,128)(2,1)})) %all-reduce.9.cloned.1.call-update) | async-done | bytes 2097168 | tf_op jit(solution)/shard_map/psum | solution.py:151
  698.0 4.0 multiply_reduce_fusion
  702.1 6.1 scatter_custom_fusion
  708.2 7.2 scatter_custom_fusion.1
  (592 shorter events, 310.4 us)
Async XLA Ops:
  7.2 245.3 %copy-start = (bf16[512,1024]{1,0:T(8,128)(2,1)S(1)}, bf16[512,1024]{1,0:T(8,128)(2,1)}, u32[]{:S(2)}) copy-start(bf16[512,1024]{1,0:T(8,128)(2,1)} %param.32) | copy-start | bytes 3145732
  7.2 243.1 %all-reduce.5.cloned.1.call-start = ((), (), s32[]{:S(2)}) async-start(), calls=%async_computation | async-start | bytes 2097152 | tf_op jit(solution)/shard_map/psum | solution.py:138
  8.6 6.0 copy-start.30
  14.0 7.9 %copy-start.13 = (bf16[1024,512]{1,0:T(8,128)(2,1)}, bf16[1024,512]{1,0:T(8,128)(2,1)S(1)}, u32[]{:S(2)}) copy-start(bf16[1024,512]{1,0:T(8,128)(2,1)S(1)} %gather_fusion) | copy-start | bytes 3145732
  14.0 6.6 copy-start.22
  15.2 17.7 %collective-permute-start.1 = (bf16[1024,512]{1,0:T(8,128)(2,1)S(1)}, bf16[1024,512]{1,0:T(8,128)(2,1)}, u32[]{:S(2)}, u32[]{:S(2)}) collective-permute-start(bf16[1024,512]{1,0:T(8,128)(2,1)S(1)} %multiply_convert_fusion.3), channel_id=1, source_target_pairs={{2,0},{4,2},{6,4},{8,6},{10,8},{12,10},{14,12},{16,14},{18,16},{20... | collective-permute-start | bytes 3145736 | tf_op jit(solution)/shard_map/ppermute | solution.py:21
  20.6 17.1 %collective-permute-start = (bf16[1024,512]{1,0:T(8,128)(2,1)S(1)}, bf16[1024,512]{1,0:T(8,128)(2,1)}, u32[]{:S(2)}, u32[]{:S(2)}) collective-permute-start(bf16[1024,512]{1,0:T(8,128)(2,1)S(1)} %multiply_convert_fusion.3), channel_id=1, source_target_pairs={{0,2},{2,4},{4,6},{6,8},{8,10},{10,12},{12,14},{14,16},{16,18},{18... | collective-permute-start | bytes 3145736 | tf_op jit(solution)/shard_map/ppermute | solution.py:18
  23.9 2.9 copy-start.32
  23.9 3.0 copy-start.34
  23.9 3.6 copy-start.25
  28.5 12.6 %copy-start.20 = (bf16[512,512]{1,0:T(8,128)(2,1)}, bf16[512,512]{1,0:T(8,128)(2,1)S(1)}, u32[]{:S(2)}) copy-start(bf16[512,512]{1,0:T(8,128)(2,1)S(1)} %constant_dynamic-update-slice_fusion) | copy-start | bytes 1572868
  204.3 99.3 %all-reduce.7.cloned.1.call-start = ((), (), s32[]{:S(2)}) async-start(), calls=%async_computation.1 | async-start | bytes 2097152 | tf_op jit(solution)/shard_map/psum | solution.py:159
  209.4 43.1 %copy-start.28 = (f32[512]{0:T(512)S(1)}, f32[512]{0:T(512)}, u32[]{:S(2)}) copy-start(f32[512]{0:T(512)} %param.31) | copy-start | bytes 6148
  252.5 53.0 %copy-start.7 = (f32[1024,512]{1,0:T(8,128)}, f32[1024,512]{1,0:T(8,128)S(1)}, u32[]{:S(2)}) copy-start(f32[1024,512]{1,0:T(8,128)S(1)} %get-tuple-element.343) | copy-start | bytes 6291460
  263.4 42.1 %copy-start.18 = (bf16[1024,512]{1,0:T(8,128)(2,1)S(1)}, bf16[1024,512]{1,0:T(8,128)(2,1)}, u32[]{:S(2)}) copy-start(bf16[1024,512]{1,0:T(8,128)(2,1)} %gather_fusion.1) | copy-start | bytes 3145732
  263.4 434.6 %all-reduce.9.cloned.1.call-start = ((), (), s32[]{:S(2)}) async-start(), calls=%async_computation.2 | async-start | bytes 4194304 | tf_op jit(solution)/shard_map/psum | solution.py:151
  318.9 2.4 copy-start.9
  319.3 3.2 copy-start.5
  342.1 2.4 copy-start.9
  342.5 3.2 copy-start.5
  365.3 2.4 copy-start.9
  365.7 3.2 copy-start.5
  388.5 2.4 copy-start.9
  388.9 3.2 copy-start.5
  411.7 2.4 copy-start.9
  412.1 3.2 copy-start.5
  434.9 2.4 copy-start.9
  435.3 3.2 copy-start.5
  458.1 2.4 copy-start.9
  458.5 3.2 copy-start.5
  481.3 2.4 copy-start.9
  481.7 3.2 copy-start.5
  504.9 3.2 copy-start.5
  528.1 3.2 copy-start.5
  551.3 3.2 copy-start.5
  574.5 3.2 copy-start.5
  594.0 6.5 copy-start.21
  600.5 10.4 %copy-start.33 = (bf16[1024,512]{1,0:T(8,128)(2,1)S(1)}, bf16[1024,512]{1,0:T(8,128)(2,1)}, u32[]{:S(2)}) copy-start(bf16[1024,512]{1,0:T(8,128)(2,1)} %param.33) | copy-start | bytes 3145732
  606.0 4.9 copy-start.16
  606.2 17.1 %collective-permute-start.3 = (bf16[1024,512]{1,0:T(8,128)(2,1)S(1)}, bf16[1024,512]{1,0:T(8,128)(2,1)S(1)}, u32[]{:S(2)}, u32[]{:S(2)}) collective-permute-start(bf16[1024,512]{1,0:T(8,128)(2,1)S(1)} %get-tuple-element.353), channel_id=1, source_target_pairs={{0,2},{2,4},{4,6},{6,8},{8,10},{10,12},{12,14},{14,16},{16,18},{18... | collective-permute-start | bytes 3145736 | tf_op jit(solution)/shard_map/ppermute | solution.py:29
  606.3 7.1 copy-start.12
  606.3 17.0 %collective-permute-start.2 = (bf16[1024,512]{1,0:T(8,128)(2,1)S(1)}, bf16[1024,512]{1,0:T(8,128)(2,1)S(1)}, u32[]{:S(2)}, u32[]{:S(2)}) collective-permute-start(bf16[1024,512]{1,0:T(8,128)(2,1)S(1)} %get-tuple-element.352), channel_id=1, source_target_pairs={{0,30},{2,0},{4,2},{6,4},{8,6},{10,8},{12,10},{14,12},{16,14},{18,... | collective-permute-start | bytes 3145736 | tf_op jit(solution)/shard_map/ppermute | solution.py:29
  613.4 9.9 %copy-start.23 = (bf16[512,256]{1,0:T(8,128)(2,1)S(1)}, bf16[512,256]{1,0:T(8,128)(2,1)}, u32[]{:S(2)}) copy-start(bf16[512,256]{1,0:T(8,128)(2,1)} %param.27) | copy-start | bytes 786436
  626.3 71.7 %copy-start.14 = (bf16[1024,512]{1,0:T(8,128)(2,1)S(1)}, bf16[1024,512]{1,0:T(8,128)(2,1)}, u32[]{:S(2)}) copy-start(bf16[1024,512]{1,0:T(8,128)(2,1)} %copy-done.13) | copy-start | bytes 3145732
  626.3 71.7 %copy-start.27 = (f32[1024]{0:T(1024)S(1)}, f32[1024]{0:T(1024)}, u32[]{:S(2)}) copy-start(f32[1024]{0:T(1024)} %copy-done.26) | copy-start | bytes 12292
  626.3 71.7 %copy-start.31 = (f32[512]{0:T(512)S(1)}, f32[512]{0:T(512)}, u32[]{:S(2)}) copy-start(f32[512]{0:T(512)} %param.26) | copy-start | bytes 6148
  698.0 4.0 copy-start.8
  708.2 7.2 copy-start.1
  (60 other events, 105.8 us)
Sparse Core Ops, SparseCore 0:
  204.4 45.7 all-reduce.4
  263.6 40.0 all-reduce.6
  626.5 71.5 all-reduce.8
where the time goes:
time: 734 us; the launch traced here: 722 us
  matrix products  348 us (47%)
  waiting for transfers between devices  171 us (23%)
  local copies, waits for them, and re-layouts  117 us (16%)
  other arithmetic  33.7 us (5%)
  loops' own time  27.4 us (4%)
  between operations  14.6 us (2%)
  starting transfers between devices  10.4 us (1%)
    dot_general x36, matrix products, slot_scores(): jnp.einsum('bc,ckf->bkf', table.astype(jnp.bfloat16), pair_blocks, prefer...  91.6 us
    dot_general x12, matrix products, back_step(): jnp.einsum('bc,bkf->ckf', table.astype(jnp.float32), portion, precision=h...  80.6 us
    psum x1, waiting for transfers between devices, local(): lax.psum(ffn_terms.astype(jnp.bfloat16), 'head').astype(jnp.float32)  71.7 us
    dot_general x12, matrix products, output_step(): jnp.einsum('bhqk,bkhd->bqhd', attn_probs, value_tile_blocks, preferred_el...  44.3 us
    psum x1, waiting for transfers between devices, local(): lax.psum(jnp.dot(attended_output, out_weight, preferred_element_type=jnp....  40.8 us
    psum x1, waiting for transfers between devices, local(): lax.psum(jnp.dot(grad_pre, ffn_in.T, preferred_element_type=jnp.float32)....  40 us
    dot_general x24, matrix products, slot_scores(): jnp.einsum('bqhd,bkhd->bhqk', query_blocks, key_tile_blocks, preferred_el...  32.1 us
    slice x36, local copies, waits for them, and re-layouts, slot_scores(): tiles[:, :, col_share:].reshape(block_count, block_len, local_heads, HD)  29.8 us
  transfers between devices with their start and end apart: 7, of which 6 were waited for; matrix products, arithmetic and copies ran while one was open for 2% of the time, Pallas kernels for 0%

commit v1 on v0

v1 whole, which is shorter than its diff:
```python
import functools

import jax
import jax.numpy as jnp
from jax import lax
from jax.experimental import pallas as pl
from jax.experimental.pallas import tpu as pltpu
from jax.sharding import PartitionSpec as P

HD = 64
PAIR = 2 * HD
EPSILON = 1e-05
F32 = jnp.float32
BF16 = jnp.bfloat16
VMEM = pl.BlockSpec(memory_space=pltpu.VMEM)
SMEM = pl.BlockSpec(memory_space=pltpu.SMEM)
COUNT_COL = 12
BLOCK_COL = 13
GROUP_COL = 14
OWN_COL = 15
COST = 1000


def dot_nn(a, b):
    return lax.dot_general(a, b, (((1,), (0,)), ((), ())), preferred_element_type=F32)


def dot_nt(a, b):
    return lax.dot_general(a, b, (((1,), (1,)), ((), ())), preferred_element_type=F32)


def row_scale(values):
    return lax.rsqrt(jnp.mean(values * values, axis=-1, keepdims=True) + EPSILON)


def call(kernel, out_shape, in_specs, scratch=(), vmem=16):
    out_specs = jax.tree.map(lambda _: VMEM, out_shape)
    return pl.pallas_call(
        kernel,
        out_shape=out_shape,
        in_specs=in_specs,
        out_specs=out_specs,
        scratch_shapes=list(scratch),
        compiler_params=pltpu.CompilerParams(vmem_limit_bytes=vmem << 20),
        cost_estimate=pl.CostEstimate(flops=COST, bytes_accessed=COST, transcendentals=0),
    )


def shaped(shape, dtype):
    return jax.ShapeDtypeStruct(shape, dtype)


def column_of(row, size):
    return jnp.broadcast_to(row, (size, size)).T


def sort_matrix(pos_ref, first, size, total):
    lanes = lax.broadcasted_iota(jnp.int32, (128, total), 1).astype(F32)
    parts = []
    for start in range(first, first + size, 128):
        column = column_of(places(pos_ref, start, 128).astype(F32), 128)
        wide = jnp.concatenate([column] * (total // 128), axis=1)
        parts.append(jnp.where(wide == lanes, 1.0, 0.0).astype(BF16))
    return jnp.concatenate(parts, axis=0)


def places(pos_ref, start, size):
    return lax.rem(pos_ref[:, start : start + size], pos_ref.shape[1])


def plan_kernel(head_groups, where_ref, lists_ref, counts_ref, meta_ref):
    blocks, slots = lists_ref.shape
    region, regions, group, heads = where_ref[0], where_ref[1], where_ref[2], head_groups
    counts = [counts_ref[i] for i in range(blocks)]
    for i in range(blocks):
        rank = jnp.int32(0)
        for j in range(blocks):
            if j != i:
                ahead = counts[j] >= counts[i] if j < i else counts[j] > counts[i]
                rank = rank + jnp.where(ahead, 1, 0)
        turn = rank // heads
        side = rank % heads
        side = jnp.where(turn % 2 == 1, heads - 1 - side, side)
        from_me = group - side
        from_me = jnp.where(from_me < 0, from_me + heads, from_me)
        row = from_me * (blocks // heads) + turn
        meta_ref[row, COUNT_COL] = counts[i]
        meta_ref[row, BLOCK_COL] = jnp.int32(i)
        meta_ref[row, GROUP_COL] = group
        entries = []
        own_total = jnp.int32(0)
        for s in range(slots):
            key = lists_ref[i, s]
            away = key // blocks - region + 1
            away = jnp.where(away < 0, away + regions, away)
            away = jnp.where(away >= regions, away - regions, away)
            own = (away == 1) & (s < counts[i])
            entries.append((key % blocks + jnp.where(away == 2, blocks, 0), away == 1))
            own_total = own_total + jnp.where(own, 1, 0)
        meta_ref[row, OWN_COL] = own_total
        own_next, other_next = jnp.int32(0), own_total
        for s in range(slots):
            index, own = entries[s]

            @pl.when(s < counts[i])
            def _(index=index, own=own, own_next=own_next, other_next=other_next):
                meta_ref[row, jnp.where(own, own_next, other_next)] = index

            own_next = own_next + jnp.where(own, 1, 0)
            other_next = other_next + jnp.where(own, 0, 1)


def prep_kernel(pos_ref, rows_ref, gain_ref, normed_ref):
    total = rows_ref.shape[0]
    for first in range(0, total, 512):
        picked = dot_nn(sort_matrix(pos_ref, first, 512, total), rows_ref[...])
        normed_ref[first : first + 512, :] = (picked * row_scale(picked) * gain_ref[...]).astype(BF16)


def sort_kernel(pos_ref, rows_ref, grads_ref, sorted_rows_ref, sorted_grads_ref):
    total = rows_ref.shape[0]
    for first in range(0, total, 512):
        matrix = sort_matrix(pos_ref, first, 512, total)
        sorted_rows_ref[first : first + 512, :] = dot_nn(matrix, rows_ref[...]).astype(BF16)
        sorted_grads_ref[first : first + 512, :] = dot_nn(matrix, grads_ref[...]).astype(BF16)


def chunk(values, who, share):
    out = values[:, :share]
    for start in range(share, values.shape[1], share):
        out = jnp.where(who == start // share, values[:, start : start + share], out)
    return out


def below(group, steps, count):
    who = group + steps
    return jnp.where(who >= count, who - count, who)


def both_heads(rows):
    lane = lax.broadcasted_iota(jnp.int32, rows.shape, 1)
    zero = jnp.zeros_like(rows)
    return jnp.concatenate([jnp.where(lane < HD, rows, zero), jnp.where(lane < HD, zero, rows)], axis=0)


def own_heads(wide):
    half = wide.shape[1] // 2
    return jnp.concatenate([wide[:HD, :half], wide[HD:, half:]], axis=0)


def groups_of_eight(tile, op):
    out = tile[:8]
    for start in range(8, tile.shape[0], 8):
        out = op(out, tile[start : start + 8])
    return out


def joined(mine_ref, packs, which):
    parts = [mine_ref[...]]
    for ref in packs:
        size = ref.shape[1] // 3
        parts.append(ref[:, which * size : (which + 1) * size])
    return jnp.concatenate(parts, axis=1)


def project_keys(rows_ref, wk, wv, keys_ref, values_ref, values_t_ref, base):
    for start in range(0, rows_ref.shape[0], 512):
        at = slice(base + start, base + start + 512)
        here = rows_ref[start : start + 512, :]
        keys_ref[at, :] = dot_nn(here, wk).astype(BF16)
        found = dot_nn(here, wv).astype(BF16)
        values_ref[at, :] = found
        for part in range(4):
            values_t_ref[(base + start) // 128 + part] = found[part * 128 : part * 128 + 128, :].T


def two_slots(meta_ref, b, first, count, step):
    one = first + 2 * step
    two = jnp.minimum(one + 1, first + count - 1)
    return meta_ref[b, one], meta_ref[b, two], 2 * step + 1 < count


def block_rows(ref, index, cols):
    return ref[pl.ds(pl.multiple_of(index * 128, 128), 128), cols]


def both_rows(ref, one, two, cols):
    return jnp.concatenate([block_rows(ref, one, cols), block_rows(ref, two, cols)], axis=0)


def both_cols(ref, one, two, cols):
    return jnp.concatenate([ref[one, cols, :], ref[two, cols, :]], axis=1)


def attend(meta_ref, b, first, count, keys_ref, values_t_ref, query_t_ref, keep_ref, acc_ref, old):
    pairs = query_t_ref.shape[0]
    wide = query_t_ref.shape[2]
    steps = (count + 1) // 2

    def peak_step(i, peaks):
        one, two, _ = two_slots(meta_ref, b, first, count, i)
        out = []
        for p in range(pairs):
            cols = slice(p * PAIR, (p + 1) * PAIR)
            tile = dot_nn(both_rows(keys_ref, one, two, cols), query_t_ref[p])
            keep_ref[i, p] = tile
            out.append(jnp.maximum(peaks[p], groups_of_eight(tile, jnp.maximum)))
        return tuple(out)

    if old is None:
        start = (jnp.full((8, wide), -3.0e38, F32),) * pairs
    else:
        start = tuple(jnp.broadcast_to(peak, (8, wide)) for peak, _ in old)
    peaks = lax.fori_loop(0, steps, peak_step, start)
    peaks = tuple(jnp.max(peak, axis=0, keepdims=True) for peak in peaks)
    totals = []
    for p in range(pairs):
        if old is None:
            acc_ref[p] = jnp.zeros(acc_ref.shape[1:], F32)
            totals.append(jnp.zeros((1, wide), F32))
        else:
            shrink = jnp.exp(old[p][0] - peaks[p])
            acc_ref[p] = acc_ref[p] * shrink
            totals.append(old[p][1] * shrink)

    def sum_step(i, sums):
        one, two, live = two_slots(meta_ref, b, first, count, i)
        out = []
        for p in range(pairs):
            cols = slice(p * PAIR, (p + 1) * PAIR)
            upper = jnp.exp(keep_ref[i, p, :128] - peaks[p])
            lower = jnp.exp(keep_ref[i, p, 128:] - jnp.where(live, peaks[p], 3.0e38))
            out.append(sums[p] + groups_of_eight(upper + lower, jnp.add))
            probs = jnp.concatenate([upper, lower], axis=0).astype(BF16)
            acc_ref[p] += dot_nn(both_cols(values_t_ref, one, two, cols), probs)
        return tuple(out)

    sums = lax.fori_loop(0, steps, sum_step, (jnp.zeros((8, wide), F32),) * pairs)
    return [
        (peaks[p], totals[p] + jnp.sum(sums[p], axis=0, keepdims=True)) for p in range(pairs)
    ]


def own_kernel(
    meta_ref,
    own_ref,
    wq_ref,
    wk_ref,
    wv_ref,
    pack_a,
    pack_b,
    keys_ref,
    values_ref,
    queries_ref,
    acc_ref,
    peaks_ref,
    sums_ref,
    keep_ref,
    values_t_ref,
    query_t_ref,
):
    block = 128
    pairs = queries_ref.shape[1] // PAIR
    packs = (pack_a, pack_b)
    project_keys(own_ref, joined(wk_ref, packs, 1), joined(wv_ref, packs, 2), keys_ref, values_ref, values_t_ref, 0)
    wq = joined(wq_ref, packs, 0)

    @pl.loop(0, queries_ref.shape[0] // block)
    def _(b):
        first = pl.multiple_of(meta_ref[b, BLOCK_COL] * block, block)
        query = dot_nn(own_ref[pl.ds(first, block), :], wq).astype(BF16)
        query = (query.astype(F32) * (HD ** (-0.5))).astype(BF16)
        queries_ref[pl.ds(pl.multiple_of(b * block, block), block), :] = query
        for p in range(pairs):
            query_t_ref[p] = both_heads(query[:, p * PAIR : (p + 1) * PAIR]).T
        found = attend(
            meta_ref,
            b,
            0,
            meta_ref[b, OWN_COL],
            keys_ref,
            values_t_ref,
            query_t_ref,
            keep_ref,
            acc_ref.at[b],
            None,
        )
        for p in range(pairs):
            at = slice(p * 2 * block, (p + 1) * 2 * block)
            peaks_ref[pl.ds(b, 1), at] = found[p][0]
            sums_ref[pl.ds(b, 1), at] = found[p][1]


def halo_kernel(
    meta_ref,
    low_ref,
    high_ref,
    wk_ref,
    wv_ref,
    pack_a,
    pack_b,
    queries_ref,
    old_acc_ref,
    peaks_ref,
    sums_ref,
    keys_ref,
    values_ref,
    attended_ref,
    attended_t_ref,
    log_total_ref,
    keep_ref,
    values_t_ref,
    query_t_ref,
    acc_ref,
):
    block = 128
    pairs = queries_ref.shape[1] // PAIR
    wk = joined(wk_ref, (pack_a, pack_b), 1)
    wv = joined(wv_ref, (pack_a, pack_b), 2)
    project_keys(low_ref, wk, wv, keys_ref, values_ref, values_t_ref, 0)
    project_keys(high_ref, wk, wv, keys_ref, values_ref, values_t_ref, low_ref.shape[0])

    @pl.loop(0, queries_ref.shape[0] // block)
    def _(b):
        here = pl.ds(pl.multiple_of(b * block, block), block)
        old = []
        for p in range(pairs):
            at = slice(p * 2 * block, (p + 1) * 2 * block)
            query_t_ref[p] = both_heads(queries_ref[here, p * PAIR : (p + 1) * PAIR]).T
            acc_ref[p] = old_acc_ref[b, p]
            old.append((peaks_ref[pl.ds(b, 1), at], sums_ref[pl.ds(b, 1), at]))
        own = meta_ref[b, OWN_COL]
        found = attend(
            meta_ref,
            b,
            own,
            meta_ref[b, COUNT_COL] - own,
            keys_ref,
            values_t_ref,
            query_t_ref,
            keep_ref,
            acc_ref,
            old,
        )
        for p in range(pairs):
            peak, total = found[p]
            log_total_ref[pl.ds(b, 1), p * 2 * block : (p + 1) * 2 * block] = peak + jnp.log(total)
            rows = own_heads(acc_ref[p] * (1.0 / total)).astype(BF16)
            attended_t_ref[b, p * PAIR : (p + 1) * PAIR, :] = rows
            attended_ref[here, p * PAIR : (p + 1) * PAIR] = rows.T


GELU_A = 0.044715
GELU_B = 0.7978845608028654


def mix_rows(wo_ref, rows_a, rows_b):
    half = (rows_a.shape[1] - wo_ref.shape[0]) // 2
    return jnp.concatenate([wo_ref[...], rows_a[:half, :], rows_b[:half, :]], axis=0)


def ffn_step(norm_ref, grad_ref, up, down):
    pre = dot_nn(norm_ref[...], up)
    square = pre * pre
    inner = jnp.tanh(GELU_B * pre * (1.0 + GELU_A * square))
    gate = 0.5 * (1.0 + inner)
    active = (pre * gate).astype(BF16)
    slope = gate + (0.5 * GELU_B) * pre * (1.0 - inner * inner) * (1.0 + (3.0 * GELU_A) * square)
    grad_pre = (dot_nt(grad_ref[...], down) * slope).astype(BF16)
    return dot_nn(active, down), dot_nt(grad_pre, up)


def ffn_kernel(
    meta_ref,
    ordered_ref,
    grad_ref,
    attended_ref,
    gain_ref,
    wo_ref,
    rows_a,
    rows_b,
    in_ref,
    out_ref,
    hidden_ref,
    grad_rows,
    norm_ref,
    total_ref,
    back_ref,
):
    block = 128
    size = attended_ref.shape[0]
    for b in range(size // block):
        first = pl.multiple_of(meta_ref[b, BLOCK_COL] * block, block)
        hidden_ref[b * block : (b + 1) * block, :] = ordered_ref[pl.ds(first, block), :].astype(F32)
        grad_rows[b * block : (b + 1) * block, :] = grad_ref[pl.ds(first, block), :]
    mixing = mix_rows(wo_ref, rows_a, rows_b)
    hidden_in = hidden_ref[...] + dot_nn(attended_ref[...], mixing)
    hidden_ref[...] = hidden_in
    norm_ref[...] = (hidden_in * row_scale(hidden_in) * gain_ref[...]).astype(BF16)
    for start in range(0, in_ref.shape[1], 512):
        at = slice(start, start + 512)
        forward, backward = ffn_step(norm_ref, grad_rows, in_ref[:, at], out_ref[at, :])
        if start == 0:
            total_ref[...] = forward
            back_ref[...] = backward
        else:
            total_ref[...] += forward
            back_ref[...] += backward


def rest_kernel(
    meta_ref,
    hidden_ref,
    grad_rows,
    norm_ref,
    old_total_ref,
    old_back_ref,
    gain_ref,
    wo_ref,
    rows_a,
    rows_b,
    in_a,
    in_b,
    mixed_grad_ref,
    out_own_ref,
    hidden_own_ref,
    *refs,
):
    heads = (len(refs) - 2) // 2 + 1
    total_ref, back_ref = refs[-2:]
    forward, backward = ffn_step(norm_ref, grad_rows, in_a[...], rows_a[-in_a.shape[1] :, :])
    total_ref[...] = old_total_ref[...] + forward
    back_ref[...] = old_back_ref[...] + backward
    forward, backward = ffn_step(norm_ref, grad_rows, in_b[...], rows_b[-in_b.shape[1] :, :])
    hidden_in = hidden_ref[...]
    result = (hidden_in + (total_ref[...] + forward)).astype(BF16)
    group = meta_ref[0, GROUP_COL]
    share = out_own_ref.shape[1]
    out_own_ref[...] = chunk(result, group, share)
    for k in range(1, heads):
        refs[k - 1][...] = chunk(result, below(group, k, heads), share)
    scale = row_scale(hidden_in)
    second_norm = hidden_in * scale
    scaled = (back_ref[...] + backward) * gain_ref[...]
    hidden_grad = grad_rows[...].astype(F32) + scale * (
        scaled - second_norm * jnp.mean(scaled * second_norm, axis=-1, keepdims=True)
    )
    hidden_own_ref[...] = chunk(hidden_grad, group, share)
    for k in range(1, heads):
        refs[heads + k - 2][...] = chunk(hidden_grad, below(group, k, heads), share)
    narrow = hidden_grad.astype(BF16)
    mixed_grad_ref[...] = dot_nt(narrow, mix_rows(wo_ref, rows_a, rows_b)).astype(BF16)


def scores_back(
    meta_ref,
    b,
    first,
    count,
    keys_ref,
    values_ref,
    keys_t_ref,
    queries_ref,
    mixed_grad_ref,
    attended_t_ref,
    log_total_ref,
    grad_keys,
    grad_values,
    rows_ref,
    rows_t_ref,
    acc_ref,
):
    block = 128
    pairs = queries_ref.shape[1] // PAIR
    here = pl.ds(pl.multiple_of(b * block, block), block)
    deltas = []
    logs = []
    for p in range(pairs):
        cols = slice(p * PAIR, (p + 1) * PAIR)
        query = both_heads(queries_ref[here, cols])
        grad = both_heads(mixed_grad_ref[here, cols])
        grad_t = grad.T
        rows_ref[0, p] = query
        rows_ref[1, p] = grad
        rows_t_ref[0, p] = query.T
        rows_t_ref[1, p] = grad_t
        attended = attended_t_ref[b, cols, :].astype(F32)
        product = grad_t.astype(F32) * jnp.concatenate([attended, attended], axis=1)
        deltas.append(jnp.sum(product, axis=0, keepdims=True))
        logs.append(log_total_ref[pl.ds(b, 1), p * 2 * block : (p + 1) * 2 * block])

    @pl.loop(0, (count + 1) // 2)
    def _(i):
        one, two, live = two_slots(meta_ref, b, first, count, i)
        at_one = pl.ds(pl.multiple_of(one * block, block), block)
        at_two = pl.ds(pl.multiple_of(two * block, block), block)
        for p in range(pairs):
            cols = slice(p * PAIR, (p + 1) * PAIR)
            scores = dot_nn(both_rows(keys_ref, one, two, cols), rows_t_ref[0, p])
            upper = jnp.exp(scores[:block] - logs[p])
            lower = jnp.exp(scores[block:] - jnp.where(live, logs[p], 3.0e38))
            probs = jnp.concatenate([upper, lower], axis=0)
            prob_grad = dot_nn(both_rows(values_ref, one, two, cols), rows_t_ref[1, p])
            score_grad = (probs * (prob_grad - deltas[p])).astype(BF16)
            to_values = dot_nn(probs.astype(BF16), rows_ref[1, p])
            to_keys = dot_nn(score_grad, rows_ref[0, p])
            acc_ref[p] += dot_nn(both_cols(keys_t_ref, one, two, cols), score_grad)
            grad_values[at_one, cols] += to_values[:block]
            grad_keys[at_one, cols] += to_keys[:block]
            grad_values[at_two, cols] += to_values[block:]
            grad_keys[at_two, cols] += to_keys[block:]


def clear_back(keys_ref, keys_t_ref, grad_keys, grad_values):
    @pl.loop(0, keys_ref.shape[0] // 128)
    def _(kb):
        at = pl.ds(pl.multiple_of(kb * 128, 128), 128)
        grad_keys[at, :] = jnp.zeros((128, grad_keys.shape[1]), F32)
        grad_values[at, :] = jnp.zeros((128, grad_keys.shape[1]), F32)
        keys_t_ref[kb] = keys_ref[at, :].T


def project_back(grad_keys, grad_values, wk, wv, start, size):
    at = slice(start, start + size)
    keys_part = dot_nt(grad_keys[at, :].astype(BF16), wk)
    return keys_part + dot_nt(grad_values[at, :].astype(BF16), wv)


def halo_back_kernel(
    meta_ref,
    keys_ref,
    values_ref,
    queries_ref,
    mixed_grad_ref,
    attended_t_ref,
    log_total_ref,
    wk_ref,
    wv_ref,
    pack_a,
    pack_b,
    low_ref,
    high_ref,
    acc_ref,
    grad_keys,
    grad_values,
    keys_t_ref,
    rows_ref,
    rows_t_ref,
):
    rows = low_ref.shape[0]
    clear_back(keys_ref, keys_t_ref, grad_keys, grad_values)

    @pl.loop(0, queries_ref.shape[0] // 128)
    def _(b):
        own = meta_ref[b, OWN_COL]
        acc_ref[b] = jnp.zeros(acc_ref.shape[1:], F32)
        scores_back(
            meta_ref,
            b,
            own,
            meta_ref[b, COUNT_COL] - own,
            keys_ref,
            values_ref,
            keys_t_ref,
            queries_ref,
            mixed_grad_ref,
            attended_t_ref,
            log_total_ref,
            grad_keys,
            grad_values,
            rows_ref,
            rows_t_ref,
            acc_ref.at[b],
        )

    packs = (pack_a, pack_b)
    weights = joined(wk_ref, packs, 1), joined(wv_ref, packs, 2)
    for start in range(0, rows, 512):
        at = slice(start, start + 512)
        low_ref[at, :] = project_back(grad_keys, grad_values, *weights, start, 512).astype(BF16)
        high_ref[at, :] = project_back(grad_keys, grad_values, *weights, rows + start, 512).astype(BF16)


def own_back_kernel(
    meta_ref,
    keys_ref,
    values_ref,
    queries_ref,
    mixed_grad_ref,
    attended_t_ref,
    log_total_ref,
    old_acc_ref,
    wq_ref,
    wk_ref,
    wv_ref,
    pack_a,
    pack_b,
    own_ref,
    grad_keys,
    grad_values,
    keys_t_ref,
    rows_ref,
    rows_t_ref,
    acc_ref,
    query_grad,
):
    block = 128
    rows = own_ref.shape[0]
    pairs = queries_ref.shape[1] // PAIR
    blocks = queries_ref.shape[0] // block
    clear_back(keys_ref, keys_t_ref, grad_keys, grad_values)

    @pl.loop(0, blocks)
    def _(b):
        acc_ref[...] = old_acc_ref[b]
        scores_back(
            meta_ref,
            b,
            0,
            meta_ref[b, OWN_COL],
            keys_ref,
            values_ref,
            keys_t_ref,
            queries_ref,
            mixed_grad_ref,
            attended_t_ref,
            log_total_ref,
            grad_keys,
            grad_values,
            rows_ref,
            rows_t_ref,
            acc_ref,
        )
        for p in range(pairs):
            found = own_heads(acc_ref[p]) * (HD ** (-0.5))
            query_grad[pl.ds(pl.multiple_of(b * block, block), block), p * PAIR : (p + 1) * PAIR] = found.T.astype(BF16)

    packs = (pack_a, pack_b)
    weights = joined(wk_ref, packs, 1), joined(wv_ref, packs, 2)
    for start in range(0, rows, 512):
        own_ref[start : start + 512, :] = project_back(grad_keys, grad_values, *weights, start, 512)
    parts = dot_nt(query_grad[...], joined(wq_ref, packs, 0))
    for b in range(blocks):
        first = pl.multiple_of(meta_ref[b, BLOCK_COL] * block, block)
        own_ref[pl.ds(first, block), :] += parts[b * block : (b + 1) * block]


def term_kernel(meta_ref, own_ref, low_ref, high_ref, ordered_ref, gain_ref, term_ref, dots_ref, *send_refs):
    rows = own_ref.shape[0]
    share = term_ref.shape[1]
    heads = len(send_refs) + 1
    group = meta_ref[0, GROUP_COL]
    dot_rows = []
    for start in range(0, rows, 128):
        at = slice(start, start + 128)
        term = own_ref[at, :] + low_ref[at, :].astype(F32) + high_ref[at, :].astype(F32)
        ordered = ordered_ref[at, :].astype(F32)
        norm = ordered * row_scale(ordered)
        dots = jnp.sum(term * gain_ref[...] * norm, axis=-1, keepdims=True)
        dot_rows.append(jnp.broadcast_to(dots, (128, 128)).T[:1])
        term_ref[at, :] = chunk(term, group, share)
        for k in range(1, heads):
            send_refs[k - 1][at, :] = chunk(term, below(group, k, heads), share).astype(BF16)
    dots = jnp.concatenate(dot_rows, axis=0)
    dots_ref[...] = dots
    high = dots.astype(BF16)
    low = (dots - high.astype(F32)).astype(BF16)
    wide = min(share, 128)
    tail = jnp.concatenate(
        [half[:, start : start + wide] for half in (high, low) for start in range(0, 128, wide)], axis=0
    )
    if share > wide:
        tail = jnp.concatenate([tail] * (share // wide), axis=1)
    for ref in send_refs:
        ref[rows:, :] = tail


def dots_of(tail):
    wide = min(tail.shape[1], 128)
    count = 128 // wide
    size = tail.shape[0] // (2 * count)
    parts = [tail[i * size : (i + 1) * size, :wide].astype(F32) for i in range(2 * count)]
    sums = [parts[i] + parts[count + i] for i in range(count)]
    return sums[0] if count == 1 else jnp.concatenate(sums, axis=1)


def back_matrix(pos_ref, first, size, total):
    place = lax.broadcasted_iota(jnp.int32, (size, total), 0) + first
    return jnp.where(jnp.broadcast_to(places(pos_ref, 0, total), (size, total)) == place, 1.0, 0.0).astype(BF16)


def place_blocks(meta_ref, refs, all_ref):
    block = 128
    blocks = refs[0].shape[0] // block
    for k, ref in enumerate(refs):
        for b in range(blocks):
            first = pl.multiple_of(meta_ref[k * blocks + b, BLOCK_COL] * block, block)
            all_ref[pl.ds(first, block), :] = ref[b * block : (b + 1) * block, :]


def output_kernel(meta_ref, pos_ref, *refs):
    out_ref, all_ref = refs[-2:]
    place_blocks(meta_ref, refs[:-2], all_ref)
    total = all_ref.shape[0]
    for first in range(0, total, 512):
        out_ref[first : first + 512, :] = dot_nn(
            back_matrix(pos_ref, first, 512, total), all_ref[...]
        ).astype(BF16)


def final_kernel(meta_ref, pos_ref, term_ref, dots_ref, ordered_ref, gain_ref, *refs):
    out_ref, all_ref, split_ref = refs[-3:]
    heads = (len(refs) - 3 + 1) // 2
    place_blocks(meta_ref, refs[:heads], all_ref)
    got_refs = refs[heads:-3]
    total, share = out_ref.shape
    group = meta_ref[0, GROUP_COL]
    gain = chunk(gain_ref[...], group, share)
    dots = dots_ref[...]
    for ref in got_refs:
        dots = dots + dots_of(ref[total:, :])
    dots = dots * (1.0 / ordered_ref.shape[1])
    for start in range(0, total, 128):
        at = slice(start, start + 128)
        ordered = ordered_ref[at, :].astype(F32)
        scale = row_scale(ordered)
        part = chunk(ordered, group, share) * scale
        mean = column_of(dots[start // 128 : start // 128 + 1], 128)[:, :1]
        term = term_ref[at, :]
        for ref in got_refs:
            term = term + ref[at, :].astype(F32)
        value = all_ref[at, :] + scale * (term * gain - part * mean)
        high = value.astype(BF16)
        split_ref[at, :share] = high
        split_ref[at, share:] = (value - high.astype(F32)).astype(BF16)
    for first in range(0, total, 512):
        found = dot_nn(back_matrix(pos_ref, first, 512, total), split_ref[...])
        out_ref[first : first + 512, :] = found[:, :share] + found[:, share:]


def local(
    features,
    out_grad,
    bin_order,
    key_lists,
    list_counts,
    attn_gain,
    query_weight,
    key_weight,
    value_weight,
    out_weight,
    ffn_gain,
    ffn_in,
    ffn_out,
):
    rows, width = features.shape
    block_count, slots = key_lists.shape
    block = rows // block_count
    share = query_weight.shape[1]
    hidden = ffn_in.shape[1]
    region = lax.axis_index("elem")
    regions = lax.axis_size("elem")
    group = lax.axis_index("head")
    head_groups = lax.axis_size("head")
    half_count = block_count // head_groups
    mine_rows = rows // head_groups
    forward = [(i, (i + 1) % regions) for i in range(regions)]
    backward = [(target, source) for source, target in forward]
    sibling = [(i, i ^ 1) for i in range(regions)]

    def exchanged(pieces):
        return [
            lax.ppermute(piece, "head", [(i, (i + k) % head_groups) for i in range(head_groups)])
            for k, piece in enumerate(pieces, 1)
        ]

    positions = bin_order.reshape(1, rows)
    gain_one = attn_gain.reshape(1, width)
    gain_two = ffn_gain.reshape(1, width)

    normed = call(prep_kernel, shaped((rows, width), BF16), [VMEM] * 3)(positions, features, gain_one)
    low = lax.ppermute(normed, "elem", forward)
    high = lax.ppermute(normed, "elem", backward)
    projections = (query_weight, key_weight, value_weight)
    if head_groups == 2:

        def my_piece(weight, core, dim):
            size = weight.shape[dim] // 2
            return lax.dynamic_slice_in_dim(weight, core * size, size, dim)

        core, normed = lax.optimization_barrier((region % 2, normed))
        pack = jnp.concatenate([my_piece(w, core, 1) for w in projections], axis=1)
        core, pack = lax.optimization_barrier((core, pack))
        (pack_a,) = exchanged([pack])
        pack_b = lax.ppermute(pack_a, "elem", sibling)
        pack = jnp.concatenate([my_piece(out_weight, core, 0), my_piece(ffn_out, core, 0)], axis=0)
        core, pack = lax.optimization_barrier((core, pack))
        (rows_a,) = exchanged([pack])
        (up_a,) = exchanged([my_piece(ffn_in, core, 1)])
    else:

        def pieces(weight, dim):
            size = weight.shape[dim] * head_groups // 4
            whole = lax.all_gather(weight, "head", axis=dim, tiled=True)
            return jnp.split(whole, (2 * size, 3 * size), axis=dim)

        split = [pieces(w, 1) for w in projections]
        projections = tuple(parts[0] for parts in split)
        pack_a, pack_b = (jnp.concatenate([parts[i] for parts in split], axis=1) for i in (1, 2))
        mix_parts, out_parts = pieces(out_weight, 0), pieces(ffn_out, 0)
        out_weight, ffn_out = mix_parts[0], out_parts[0]
        rows_a, rows_b = (jnp.concatenate([mix_parts[i], out_parts[i]], axis=0) for i in (1, 2))
        ffn_in, up_a, up_b = pieces(ffn_in, 1)

    meta = pl.pallas_call(
        functools.partial(plan_kernel, head_groups),
        out_shape=shaped((block_count, 16), jnp.int32),
        in_specs=[SMEM] * 3,
        out_specs=SMEM,
    )(jnp.stack([region, jnp.int32(regions), group, group]), key_lists, list_counts)

    ordered, grad_sorted = call(
        sort_kernel, (shaped((rows, width), BF16), shaped((rows, width), BF16)), [VMEM] * 3
    )(positions, features, out_grad)

    heads_width = head_groups * share
    key_value = (*projections[1:], pack_a, pack_b)
    pairs = heads_width // PAIR
    pair_tile = (pairs, PAIR, 2 * block)
    keep = pltpu.VMEM(((slots + 1) // 2, pairs, 2 * block, 2 * block), F32)
    stats = shaped((half_count, 2 * heads_width), F32)
    keys, values, queries, part_acc, part_peaks, part_sums = call(
        own_kernel,
        (
            shaped((rows, heads_width), BF16),
            shaped((rows, heads_width), BF16),
            shaped((mine_rows, heads_width), BF16),
            shaped((half_count,) + pair_tile, F32),
            stats,
            stats,
        ),
        [SMEM] + [VMEM] * 6,
        scratch=(
            keep,
            pltpu.VMEM((block_count, heads_width, block), BF16),
            pltpu.VMEM(pair_tile, BF16),
        ),
        vmem=26,
    )(meta, normed, *projections, pack_a, pack_b)
    if head_groups == 2:
        queries, rows_a = lax.optimization_barrier((queries, rows_a))
        rows_b = lax.ppermute(rows_a, "elem", sibling)
    halo_keys, halo_values, attended, attended_t, log_total = call(
        halo_kernel,
        (
            shaped((2 * rows, heads_width), BF16),
            shaped((2 * rows, heads_width), BF16),
            shaped((mine_rows, heads_width), BF16),
            shaped((half_count, heads_width, block), BF16),
            stats,
        ),
        [SMEM] + [VMEM] * 10,
        scratch=(
            keep,
            pltpu.VMEM((2 * block_count, heads_width, block), BF16),
            pltpu.VMEM(pair_tile, BF16),
            pltpu.VMEM(pair_tile, F32),
        ),
        vmem=30,
    )(meta, low, high, *key_value, queries, part_acc, part_peaks, part_sums)

    square = shaped((mine_rows, width), F32)
    narrow = shaped((mine_rows, width), BF16)
    if head_groups == 2:
        attended, up_a = lax.optimization_barrier((attended, up_a))
        up_b = lax.ppermute(up_a, "elem", sibling)
    hidden_in, grad_rows, norm_two, part_total, part_back = call(
        ffn_kernel,
        (square, narrow, narrow, square, square),
        [SMEM] + [VMEM] * 9,
    )(meta, ordered, grad_sorted, attended, gain_two, out_weight, rows_a, rows_b, ffn_in, ffn_out)
    others = head_groups - 1
    mixed_grad, out_own, hidden_own, *sends = call(
        rest_kernel,
        (
            narrow,
            shaped((mine_rows, share), BF16),
            shaped((mine_rows, share), F32),
            *[shaped((mine_rows, share), BF16)] * others,
            *[shaped((mine_rows, share), F32)] * others,
        ),
        [SMEM] + [VMEM] * 11,
        scratch=(pltpu.VMEM((mine_rows, width), F32), pltpu.VMEM((mine_rows, width), F32)),
    )(
        meta,
        hidden_in,
        grad_rows,
        norm_two,
        part_total,
        part_back,
        gain_two,
        out_weight,
        rows_a,
        rows_b,
        up_a,
        up_b,
    )
    out_got = exchanged(sends[:others])
    hidden_got = exchanged(sends[others:])

    rows_pair = pltpu.VMEM((2, pairs, 2 * block, PAIR), BF16)
    cols_pair = pltpu.VMEM((2,) + pair_tile, BF16)
    grad_low, grad_high, part_grad = call(
        halo_back_kernel,
        (
            shaped((rows, width), BF16),
            shaped((rows, width), BF16),
            shaped((half_count,) + pair_tile, F32),
        ),
        [SMEM] + [VMEM] * 10,
        scratch=(
            pltpu.VMEM((2 * rows, heads_width), F32),
            pltpu.VMEM((2 * rows, heads_width), F32),
            pltpu.VMEM((2 * block_count, heads_width, block), BF16),
            rows_pair,
            cols_pair,
        ),
        vmem=36,
    )(meta, halo_keys, halo_values, queries, mixed_grad, attended_t, log_total, *key_value)
    from_right = lax.ppermute(grad_low, "elem", backward)
    from_left = lax.ppermute(grad_high, "elem", forward)
    grad_own = call(
        own_back_kernel,
        shaped((rows, width), F32),
        [SMEM] + [VMEM] * 12,
        scratch=(
            pltpu.VMEM((rows, heads_width), F32),
            pltpu.VMEM((rows, heads_width), F32),
            pltpu.VMEM((block_count, heads_width, block), BF16),
            rows_pair,
            cols_pair,
            pltpu.VMEM(pair_tile, F32),
            pltpu.VMEM((mine_rows, heads_width), BF16),
        ),
        vmem=30,
    )(
        meta,
        keys,
        values,
        queries,
        mixed_grad,
        attended_t,
        log_total,
        part_grad,
        *projections,
        pack_a,
        pack_b,
    )
    from_right, from_left, out_got, hidden_got = lax.optimization_barrier(
        (from_right, from_left, out_got, hidden_got)
    )
    tail = 2 * (rows // 128) * (128 // min(share, 128))
    term, dots, *sends = call(
        term_kernel,
        (
            shaped((rows, share), F32),
            shaped((rows // 128, 128), F32),
            *[shaped((rows + tail, share), BF16)] * others,
        ),
        [SMEM] + [VMEM] * 5,
    )(meta, grad_own, from_right, from_left, ordered, gain_one)
    got = exchanged(sends)
    output = call(
        output_kernel,
        shaped((rows, share), BF16),
        [SMEM] + [VMEM] * (1 + head_groups),
        scratch=(pltpu.VMEM((rows, share), BF16),),
    )(meta, positions, out_own, *out_got)
    input_grad = call(
        final_kernel,
        shaped((rows, share), F32),
        [SMEM] + [VMEM] * (4 + 2 * head_groups),
        scratch=(pltpu.VMEM((rows, share), F32), pltpu.VMEM((rows, 2 * share), BF16)),
    )(meta, positions, term, dots, ordered, gain_one, hidden_own, *hidden_got, *got)
    return (output, input_grad)


def solution(mesh):
    in_specs = (
        P("elem", None),
        P("elem", None),
        P("elem"),
        P("elem", None),
        P("elem"),
        P(),
        P(None, "head"),
        P(None, "head"),
        P(None, "head"),
        P("head", None),
        P(),
        P(None, "head"),
        P("head", None),
    )
    out_specs = (P("elem", "head"), P("elem", "head"))
    return jax.shard_map(local, mesh=mesh, in_specs=in_specs, out_specs=out_specs, check_vma=False)
```

time: 734 us -> 122 us (0.17); the launches traced: 722 us -> 120 us
  matrix products: 348 us -> 0 us
  waiting for transfers between devices: 171 us -> 26.5 us
  local copies, waits for them, and re-layouts: 117 us -> 5.98 us
  Pallas kernels: 0 us -> 71.5 us
  other arithmetic: 33.7 us -> 3.17 us
  loops' own time: 27.4 us -> 0 us
  between operations: 14.6 us -> 0.95 us
    dot_general x141 -> x0, matrix products: 348 us -> none  [the longest x36 91.6 us: slot_scores(): jnp.einsum('bc,ckf->bkf', table.astype(jnp.bfloat16), pair_blocks, prefer...]
    psum x3 -> x0, waiting for transfers between devices: 152 us -> none  [the longest x1 71.7 us: local(): lax.psum(ffn_terms.astype(jnp.bfloat16), 'head').astype(jnp.float32)]
    pallas_call x0 -> x12, Pallas kernels: none -> 71.5 us  [the longest x1 17.6 us: local(): call(halo_back_kernel, (shaped((rows, width), BF16), shaped((rows, width)...]
    slice x97 -> x0, local copies, waits for them, and re-layouts: 46.8 us -> none  [the longest x36 29.8 us: slot_scores(): tiles[:, :, col_share:].reshape(block_count, block_len, local_heads, HD)]
    another operation x3 -> x0, loops' own time: 27.4 us -> none  [the longest x1 9.91 us: local(): lax.fori_loop(0, top_count, back_step, (zero_query, zero_wide))]
    reshape x25 -> x0, local copies, waits for them, and re-layouts: 26.2 us -> none  [the longest x12 20.3 us: back_step(): value_portion.reshape(block_count, block_len, col_share)]
    reduce_sum x16 -> x0, other arithmetic: 15.4 us -> none  [the longest x11 6.24 us: stats_step(): jnp.sum(jnp.exp(attention_scores - new_max[..., None]), axis=-1)]
    while x157 -> x0, local copies, waits for them, and re-layouts: 14.1 us -> none  [the longest x2 7.1 us: local(): lax.fori_loop(0, top_count, back_step, (zero_query, zero_wide))]
  transfers between devices with their start and end apart: 7 -> 13, of which waited for: 6 -> 3; matrix products, arithmetic and copies ran while one was open for 2% -> 5% of each run, Pallas kernels for 0% -> 35%
where the time goes in v1:
time: 122 us; the launch traced here: 120 us
  Pallas kernels  71.5 us (59%)
  waiting for transfers between devices  26.5 us (22%)
  starting transfers between devices  12.3 us (10%)
  local copies, waits for them, and re-layouts  5.98 us (5%)
  other arithmetic  3.17 us (3%)
    ppermute x6, waiting for transfers between devices, exchanged(): lax.ppermute(piece, 'head', [(i, (i + k) % head_groups) for i in range(he...  26.5 us
    pallas_call x1, Pallas kernels, local(): call(halo_back_kernel, (shaped((rows, width), BF16), shaped((rows, width)...  17.6 us
    pallas_call x1, Pallas kernels, local(): call(halo_kernel, (shaped((2 * rows, heads_width), BF16), shaped((2 * row...  12.3 us
    pallas_call x1, Pallas kernels, local(): call(own_back_kernel, shaped((rows, width), F32), [SMEM] + [VMEM] * 12, s...  10.8 us
    pallas_call x1, Pallas kernels, local(): call(own_kernel, (shaped((rows, heads_width), BF16), shaped((rows, heads_...  7.51 us
    ppermute x6, starting transfers between devices, exchanged(): lax.ppermute(piece, 'head', [(i, (i + k) % head_groups) for i in range(he...  5.92 us
    ppermute x1, starting transfers between devices, local(): high = lax.ppermute(normed, 'elem', backward)  5.46 us
    pallas_call x1, Pallas kernels, local(): call(rest_kernel, (narrow, shaped((mine_rows, share), BF16), shaped((mine...  4.96 us
  transfers between devices with their start and end apart: 13, of which 3 were waited for; matrix products, arithmetic and copies ran while one was open for 5% of the time, Pallas kernels for 35%

profile of v1, /device:TPU:0, one launch (start us, length us, event | category | flops | bytes accessed | tf_op | source)
XLA Modules:
  0.0 120.4 jit_solution(13114289411862830815)
XLA Ops:
  0.7 0.0 copy-start.2
  0.7 1.3 %copy-done.2 = bf16[1024,512]{1,0:T(8,128)(2,1)S(1)} copy-done((bf16[1024,512]{1,0:T(8,128)(2,1)S(1)}, bf16[1024,512]{1,0:T(8,128)(2,1)}, u32[]{:S(2)}) %copy-start.2) | copy-done | bytes 1048600
  1.9 0.7 copy-done.12
  2.6 0.7 copy-done.14
  3.3 1.4 %shard_map.142.own_ref = bf16[1024,512]{1,0:T(8,128)(2,1)S(1)} custom-call(s32[1,1024]{1,0:T(1,128)S(1)} %bitcast.5, bf16[1024,512]{1,0:T(8,128)(2,1)S(1)} %copy-done.2, f32[1,512]{1,0:T(1,128)S(1)} %bitcast.9), custom_call_target="tpu_custom_call" | custom-call | flops 1000 | bytes 1000 | tf_op jit(solution)/shard_map/pallas_call | solution.py:781
  4.8 5.5 %collective-permute-start.1 = (bf16[1024,512]{1,0:T(8,128)(2,1)S(1)}, bf16[1024,512]{1,0:T(8,128)(2,1)}, u32[]{:S(2)}, u32[]{:S(2)}) collective-permute-start(bf16[1024,512]{1,0:T(8,128)(2,1)S(1)} %shard_map.142.own_ref), channel_id=1, source_target_pairs={{2,0},{4,2},{6,4},{8,6},{10,8},{12,10},{14,12},{16,14},{18,16},{20... | collective-permute-start | bytes 3145736 | tf_op jit(solution)/shard_map/ppermute | solution.py:783
  10.2 0.0 collective-permute-start
  10.3 0.8 pad_maximum_fusion.1
  11.1 1.5 %collective-permute-start.2 = (bf16[512,384]{1,0:T(8,128)(2,1)}, bf16[512,384]{1,0:T(8,128)(2,1)S(1)}, u32[]{:S(2)}, u32[]{:S(2)}) collective-permute-start(bf16[512,384]{1,0:T(8,128)(2,1)} %pad_maximum_fusion.1), channel_id=1, source_target_pairs={{0,1},{1,0},{2,3},{3,2},{4,5},{5,4},{6,7},{7,6},{8,9},{9,8},{10,11... | collective-permute-start | bytes 1179656 | tf_op jit(solution)/shard_map/ppermute | solution.py:773
  12.6 0.7 constant_dynamic-slice_fusion.2
  13.3 1.8 %pad_maximum_fusion = bf16[640,512]{1,0:T(8,128)(2,1)} fusion(bf16[512,512]{1,0:T(8,128)(2,1)S(1)} %constant_dynamic-slice_fusion.1, bf16[128,512]{1,0:T(8,128)(2,1)} %constant_dynamic-slice_fusion.2), kind=kLoop, calls=%fused_computation | loop fusion | flops 1310720 | bytes 1310720 | tf_op jit(solution)/shard_map/concatenate | solution.py:796
  15.1 0.5 collective-permute-start.4
  15.6 7.8 %collective-permute-done.2.pack_a = bf16[512,384]{1,0:T(8,128)(2,1)S(1)} collective-permute-done((bf16[512,384]{1,0:T(8,128)(2,1)}, bf16[512,384]{1,0:T(8,128)(2,1)S(1)}, u32[]{:S(2)}, u32[]{:S(2)}) %collective-permute-start.2) | collective-permute-done | bytes 393248 | tf_op jit(solution)/shard_map/ppermute | solution.py:773
  23.4 0.0 collective-permute-start.3
  23.4 1.9 %constant_dynamic-slice_fusion = bf16[512,512]{1,0:T(8,128)(2,1)} fusion(bf16[512,1024]{1,0:T(8,128)(2,1)} %in_ref.1, s32[]{:T(128)S(6)} %select_n.25), kind=kLoop, calls=%fused_computation.2 | loop fusion | bytes 1048580 | tf_op jit(solution)/shard_map/dynamic_slice | solution.py:789
  25.2 1.5 %collective-permute-start.5 = (bf16[512,512]{1,0:T(8,128)(2,1)}, bf16[512,512]{1,0:T(8,128)(2,1)}, u32[]{:S(2)}, u32[]{:S(2)}) collective-permute-start(bf16[512,512]{1,0:T(8,128)(2,1)} %constant_dynamic-slice_fusion), channel_id=1, source_target_pairs={{0,1},{1,0},{2,3},{3,2},{4,5},{5,4},{6,7},{7,6},{8,9},{9,8},{10,11... | collective-permute-start | bytes 1572872 | tf_op jit(solution)/shard_map/ppermute | solution.py:773
  26.8 0.6 pad_add_fusion.where_ref
  27.4 3.1 %shard_map.140.meta_ref = s32[8,16]{1,0:T(8,128)} custom-call(s32[4]{0:T(128)} %pad_add_fusion.where_ref, s32[8,12]{1,0:T(8,128)} %lists_ref.1, s32[8]{0:T(128)} %counts_ref.1), custom_call_target="tpu_custom_call" | custom-call | tf_op jit(solution)/shard_map/pallas_call | solution.py:815
  30.5 0.7 copy-done.10
  31.2 7.5 %shard_map.143 = (bf16[1024,512]{1,0:T(8,128)(2,1)S(1)}, bf16[1024,512]{1,0:T(8,128)(2,1)S(1)}, bf16[512,512]{1,0:T(8,128)(2,1)S(1)}, f32[4,4,128,256]{3,2,1,0:T...) custom-call(s32[8,16]{1,0:T(8,128)S(1)} %copy-done.10, bf16[1024,512]{1,0:T(8,128)(2,1)S(1)} %shard_map.142.own_ref, ...), custom_call_target="tpu_custom_call" | custom-call | flops 1000 | bytes 1000 | tf_op jit(solution)/shard_map/pallas_call | solution.py:832
  38.7 0.0 collective-permute-done.4.rows_a
  38.7 0.3 collective-permute-start.6
  39.0 0.0 collective-permute-done.1.high_ref
  39.0 0.0 copy-start.3
  39.0 0.0 copy-start.9
  39.0 0.0 copy-start.13
  39.0 12.3 %shard_map.144 = (bf16[2048,512]{1,0:T(8,128)(2,1)S(1)}, bf16[2048,512]{1,0:T(8,128)(2,1)S(1)}, bf16[512,512]{1,0:T(8,128)(2,1)S(1)}, bf16[4,512,128]{2,1,0:T(8,128)(2,1)S(1)}, f32[4,1024]{1,0:T(4,128)S(1)}) custom-call(s32[8,16]{1,0:T(8,128)S(1)} %copy-done.11, bf16[1024,512]{1,0:T(8,128)(2,1)} %collective-permute-done.low_ref, ...), custom_call_target="tpu_custom_call" | custom-call | flops 1000 | bytes 1000 | tf_op jit(solution)/shard_map/pallas_call | solution.py:853
  51.3 0.0 copy-start.5
  51.3 0.0 copy-start.6
  51.3 0.0 copy-start.16
  51.4 0.0 collective-permute-done.5.in_a
  51.4 0.1 collective-permute-start.7
  51.5 2.4 %shard_map.141 = (bf16[1024,512]{1,0:T(8,128)(2,1)S(1)}, bf16[1024,512]{1,0:T(8,128)(2,1)S(1)}) custom-call(s32[1,1024]{1,0:T(1,128)S(1)} %bitcast.6, bf16[1024,512]{1,0:T(8,128)(2,1)S(1)} %copy-done.3, bf16[1024,512]{1,0:T(8,128)(2,1)S(1)} %copy-done.9), custom_call_target="tpu_custom_call" | custom-call | flops 1000 | bytes 1000 | tf_op jit(solution)/shard_map/pallas_call | solution.py:822
  53.9 0.0 collective-permute-done.6.rows_b
  53.9 4.1 %shard_map.145 = (f32[512,512]{1,0:T(8,128)S(1)}, bf16[512,512]{1,0:T(8,128)(2,1)S(1)}, bf16[512,512]{1,0:T(8,128)(2,1)S(1)}, f32[512,512]{1,0:T(8,128)S(1)}, f32[512,512]{1,0:T(8,128)S(1)}) custom-call(s32[8,16]{1,0:T(8,128)S(1)} %copy-done.11, bf16[1024,512]{1,0:T(8,128)(2,1)S(1)} %get-tuple-element.45.ordered_ref, ...), custom_call_target="tpu_custom_call" | custom-call | flops 1000 | bytes 1000 | tf_op jit(solution)/shard_map/pallas_call | solution.py:877
  58.0 5.0 %shard_map.146 = (bf16[512,512]{1,0:T(8,128)(2,1)S(1)}, bf16[512,256]{1,0:T(8,128)(2,1)S(1)}, f32[512,256]{1,0:T(8,128)S(1)}, bf16[512,256]{1,0:T(8,128)(2,1)S(1)}, f32[512,256]{1,0:T(8,128)S(1)}) custom-call(s32[8,16]{1,0:T(8,128)S(1)} %copy-done.11, f32[512,512]{1,0:T(8,128)S(1)} %get-tuple-element.61.hidden_ref, ...), custom_call_target="tpu_custom_call" | custom-call | flops 1000 | bytes 1000 | tf_op jit(solution)/shard_map/pallas_call | solution.py:883
  63.0 17.6 %shard_map.147 = (bf16[1024,512]{1,0:T(8,128)(2,1)S(1)}, bf16[1024,512]{1,0:T(8,128)(2,1)S(1)}, f32[4,4,128,256]{3,2,1,0:T(8,128)S(1)}) custom-call(s32[8,16]{1,0:T(8,128)S(1)} %copy-done.11, bf16[2048,512]{1,0:T(8,128)(2,1)S(1)} %get-tuple-element.68.keys_ref, bf16[2048,512]{1,0:T(8,128)(2,1)S(1)} %get-tuple-element.69.values_ref, ...), custom_call_target="tpu_custom_call" | custom-call | flops 1000 | bytes 1000 | tf_op jit(solution)/shard_map/pallas_call | solution.py:913
  80.6 0.1 collective-permute-start.8
  80.7 0.5 collective-permute-start.9
  81.2 1.1 collective-permute-start.11
  82.2 1.0 collective-permute-start.10
  83.2 10.8 %shard_map.149.own_ref = f32[1024,512]{1,0:T(8,128)S(1)} custom-call(s32[8,16]{1,0:T(8,128)S(1)} %copy-done.11, bf16[1024,512]{1,0:T(8,128)(2,1)S(1)} %get-tuple-element.78.keys_ref, bf16[1024,512]{1,0:T(8,128)(2,1)S(1)} %get-tuple-element.79.values_ref, bf16[512,512]{1,0:T(8,128)(2,1)S(1)} %get-tuple-element.53.queries_ref, ...), custom_call_target="tpu_custom_call" | custom-call | flops 1000 | bytes 1000 | tf_op jit(solution)/shard_map/pallas_call | solution.py:932
  94.0 6.6 %collective-permute-done.10.refs_1_ = bf16[512,256]{1,0:T(8,128)(2,1)S(1)} collective-permute-done((bf16[512,256]{1,0:T(8,128)(2,1)S(1)}, bf16[512,256]{1,0:T(8,128)(2,1)S(1)}, u32[]{:S(2)}, u32[]{:S(2)}) %collective-permute-start.10) | collective-permute-done | bytes 262176 | tf_op jit(solution)/shard_map/ppermute | solution.py:773
  100.6 1.7 %shard_map.150 = (f32[1024,256]{1,0:T(8,128)S(1)}, f32[8,128]{1,0:T(8,128)S(1)}, bf16[1040,256]{1,0:T(8,128)(2,1)S(1)}) custom-call(s32[8,16]{1,0:T(8,128)S(1)} %copy-done.11, f32[1024,512]{1,0:T(8,128)S(1)} %shard_map.149.own_ref, bf16[1024,512]{1,0:T(8,128)(2,1)S(1)} %collective-permute-done.8.low_ref, ...), custom_call_target="tpu_custom_call" | custom-call | flops 1000 | bytes 1000 | tf_op jit(solution)/shard_map/pallas_call | solution.py:963
  102.3 0.3 collective-permute-start.12
  102.7 2.1 %shard_map.148 = bf16[1024,256]{1,0:T(8,128)(2,1)} custom-call(s32[8,16]{1,0:T(8,128)S(1)} %copy-done.11, s32[1,1024]{1,0:T(1,128)S(1)} %bitcast.7, bf16[512,256]{1,0:T(8,128)(2,1)S(1)} %get-tuple-element.67.refs_0_, bf16[512,256]{1,0:T(8,128)(2,1)S(1)} %collective-permute-done.10.refs_1_), custom_call_target="tpu_custom_call" | custom-call | flops 1000 | bytes 1000 | tf_op jit(solution)/shard_map/pallas_call | solution.py:973
  104.8 12.1 %collective-permute-done.12.refs_2_ = bf16[1040,256]{1,0:T(8,128)(2,1)S(1)} collective-permute-done((bf16[1040,256]{1,0:T(8,128)(2,1)S(1)}, bf16[1040,256]{1,0:T(8,128)(2,1)S(1)}, u32[]{:S(2)}, u32[]{:S(2)}) %collective-permute-start.12) | collective-permute-done | bytes 532512 | tf_op jit(solution)/shard_map/ppermute | solution.py:773
  116.9 3.5 %shard_map.151 = f32[1024,256]{1,0:T(8,128)} custom-call(s32[8,16]{1,0:T(8,128)S(1)} %copy-done.11, s32[1,1024]{1,0:T(1,128)S(1)} %bitcast.8, f32[1024,256]{1,0:T(8,128)S(1)} %get-tuple-element.83.term_ref, f32[8,128]{1,0:T(8,128)S(1)} %get-tuple-element.84.dots_ref, bf16[1024,512]{1,0:T(8,128)(2,1)S(1)} %get-tuple-element.45.ordered_ref, ...), custom_call_target="tpu_custom_call" | custom-call | flops 1000 | bytes 1000 | tf_op jit(solution)/shard_map/pallas_call | solution.py:979
  (32 shorter events, 0.1 us)
Async XLA Ops:
  0.6 9.6 %copy-start.1 = (bf16[512,256]{1,0:T(8,128)(2,1)S(1)}, bf16[512,256]{1,0:T(8,128)(2,1)}, u32[]{:S(2)}) copy-start(bf16[512,256]{1,0:T(8,128)(2,1)} %wv_ref.7) | copy-start | bytes 786436
  0.6 9.6 %copy-start = (bf16[512,256]{1,0:T(8,128)(2,1)S(1)}, bf16[512,256]{1,0:T(8,128)(2,1)}, u32[]{:S(2)}) copy-start(bf16[512,256]{1,0:T(8,128)(2,1)} %wk_ref.7) | copy-start | bytes 786436
  0.7 1.3 %copy-start.2 = (bf16[1024,512]{1,0:T(8,128)(2,1)S(1)}, bf16[1024,512]{1,0:T(8,128)(2,1)}, u32[]{:S(2)}) copy-start(bf16[1024,512]{1,0:T(8,128)(2,1)} %rows_ref.3) | copy-start | bytes 3145732
  1.9 0.7 copy-start.12
  2.6 0.7 copy-start.14
  3.3 6.9 %copy-start.8 = (bf16[512,256]{1,0:T(8,128)(2,1)S(1)}, bf16[512,256]{1,0:T(8,128)(2,1)}, u32[]{:S(2)}) copy-start(bf16[512,256]{1,0:T(8,128)(2,1)} %wq_ref.3) | copy-start | bytes 786436
  3.3 9.3 %copy-start.7 = (bf16[256,512]{1,0:T(8,128)(2,1)S(1)}, bf16[256,512]{1,0:T(8,128)(2,1)}, u32[]{:S(2)}) copy-start(bf16[256,512]{1,0:T(8,128)(2,1)} %wo_ref.3) | copy-start | bytes 786436
  3.3 10.0 %copy-start.4 = (bf16[1024,512]{1,0:T(8,128)(2,1)S(1)}, bf16[1024,512]{1,0:T(8,128)(2,1)}, u32[]{:S(2)}) copy-start(bf16[1024,512]{1,0:T(8,128)(2,1)} %out_ref.1) | copy-start | bytes 3145732
  4.8 34.2 %collective-permute-start.1 = (bf16[1024,512]{1,0:T(8,128)(2,1)S(1)}, bf16[1024,512]{1,0:T(8,128)(2,1)}, u32[]{:S(2)}, u32[]{:S(2)}) collective-permute-start(bf16[1024,512]{1,0:T(8,128)(2,1)S(1)} %shard_map.142.own_ref), channel_id=1, source_target_pairs={{2,0},{4,2},{6,4},{8,6},{10,8},{12,10},{14,12},{16,14},{18,16},{20... | collective-permute-start | bytes 3145736 | tf_op jit(solution)/shard_map/ppermute | solution.py:783
  10.2 28.7 %collective-permute-start = (bf16[1024,512]{1,0:T(8,128)(2,1)S(1)}, bf16[1024,512]{1,0:T(8,128)(2,1)}, u32[]{:S(2)}, u32[]{:S(2)}) collective-permute-start(bf16[1024,512]{1,0:T(8,128)(2,1)S(1)} %shard_map.142.own_ref), channel_id=1, source_target_pairs={{0,2},{2,4},{4,6},{6,8},{8,10},{10,12},{12,14},{14,16},{16,18},{18... | collective-permute-start | bytes 3145736 | tf_op jit(solution)/shard_map/ppermute | solution.py:782
  11.1 12.3 %collective-permute-start.2 = (bf16[512,384]{1,0:T(8,128)(2,1)}, bf16[512,384]{1,0:T(8,128)(2,1)S(1)}, u32[]{:S(2)}, u32[]{:S(2)}) collective-permute-start(bf16[512,384]{1,0:T(8,128)(2,1)} %pad_maximum_fusion.1), channel_id=1, source_target_pairs={{0,1},{1,0},{2,3},{3,2},{4,5},{5,4},{6,7},{7,6},{8,9},{9,8},{10,11... | collective-permute-start | bytes 1179656 | tf_op jit(solution)/shard_map/ppermute | solution.py:773
  15.1 23.5 %collective-permute-start.4 = (bf16[640,512]{1,0:T(8,128)(2,1)}, bf16[640,512]{1,0:T(8,128)(2,1)S(1)}, u32[]{:S(2)}, u32[]{:S(2)}) collective-permute-start(bf16[640,512]{1,0:T(8,128)(2,1)} %pad_maximum_fusion), channel_id=1, source_target_pairs={{0,1},{1,0},{2,3},{3,2},{4,5},{5,4},{6,7},{7,6},{8,9},{9,8},{10,11... | collective-permute-start | bytes 1966088 | tf_op jit(solution)/shard_map/ppermute | solution.py:773
  23.4 7.1 %collective-permute-start.3 = (bf16[512,384]{1,0:T(8,128)(2,1)S(1)}, bf16[512,384]{1,0:T(8,128)(2,1)S(1)}, u32[]{:S(2)}, u32[]{:S(2)}) collective-permute-start(bf16[512,384]{1,0:T(8,128)(2,1)S(1)} %collective-permute-done.2.pack_a), channel_id=1, source_target_pairs={{0,2},{2,0},{4,6},{6,4},{8,10},{10,8},{12,14},{14,12},{16,18},{18,... | collective-permute-start | bytes 1179656 | tf_op jit(solution)/shard_map/ppermute | solution.py:795
  25.2 26.1 %collective-permute-start.5 = (bf16[512,512]{1,0:T(8,128)(2,1)}, bf16[512,512]{1,0:T(8,128)(2,1)}, u32[]{:S(2)}, u32[]{:S(2)}) collective-permute-start(bf16[512,512]{1,0:T(8,128)(2,1)} %constant_dynamic-slice_fusion), channel_id=1, source_target_pairs={{0,1},{1,0},{2,3},{3,2},{4,5},{5,4},{6,7},{7,6},{8,9},{9,8},{10,11... | collective-permute-start | bytes 1572872 | tf_op jit(solution)/shard_map/ppermute | solution.py:773
  30.5 0.7 copy-start.10
  31.2 7.8 %copy-start.11 = (s32[8,16]{1,0:T(8,128)S(1)}, s32[8,16]{1,0:T(8,128)}, u32[]{:S(2)}) copy-start(s32[8,16]{1,0:T(8,128)} %shard_map.140.meta_ref) | copy-start | bytes 1540
  38.7 15.2 %collective-permute-start.6 = (bf16[640,512]{1,0:T(8,128)(2,1)S(1)}, bf16[640,512]{1,0:T(8,128)(2,1)S(1)}, u32[]{:S(2)}, u32[]{:S(2)}) collective-permute-start(bf16[640,512]{1,0:T(8,128)(2,1)S(1)} %collective-permute-done.4.rows_a), channel_id=1, source_target_pairs={{0,2},{2,0},{4,6},{6,4},{8,10},{10,8},{12,14},{14,12},{16,18},{18,... | collective-permute-start | bytes 1966088 | tf_op jit(solution)/shard_map/ppermute | solution.py:852
  39.0 12.5 %copy-start.3 = (bf16[1024,512]{1,0:T(8,128)(2,1)S(1)}, bf16[1024,512]{1,0:T(8,128)(2,1)}, u32[]{:S(2)}) copy-start(bf16[1024,512]{1,0:T(8,128)(2,1)} %rows_ref.3) | copy-start | bytes 3145732
  39.0 12.5 %copy-start.9 = (bf16[1024,512]{1,0:T(8,128)(2,1)S(1)}, bf16[1024,512]{1,0:T(8,128)(2,1)}, u32[]{:S(2)}) copy-start(bf16[1024,512]{1,0:T(8,128)(2,1)} %grads_ref.1) | copy-start | bytes 3145732
  39.0 12.5 %copy-start.13 = (s32[1024]{0:T(1024)S(1)}, s32[1024]{0:T(1024)}, u32[]{:S(2)}) copy-start(s32[1024]{0:T(1024)} %param.15) | copy-start | bytes 12292
  51.3 2.6 %copy-start.5 = (bf16[1024,512]{1,0:T(8,128)(2,1)S(1)}, bf16[1024,512]{1,0:T(8,128)(2,1)}, u32[]{:S(2)}) copy-start(bf16[1024,512]{1,0:T(8,128)(2,1)} %out_ref.1) | copy-start | bytes 3145732
  51.3 2.6 %copy-start.6 = (bf16[512,1024]{1,0:T(8,128)(2,1)S(1)}, bf16[512,1024]{1,0:T(8,128)(2,1)}, u32[]{:S(2)}) copy-start(bf16[512,1024]{1,0:T(8,128)(2,1)} %in_ref.1) | copy-start | bytes 3145732
  51.3 2.6 %copy-start.16 = (f32[512]{0:T(512)S(1)}, f32[512]{0:T(512)}, u32[]{:S(2)}) copy-start(f32[512]{0:T(512)} %param.23) | copy-start | bytes 6148
  51.4 6.7 %collective-permute-start.7 = (bf16[512,512]{1,0:T(8,128)(2,1)}, bf16[512,512]{1,0:T(8,128)(2,1)S(1)}, u32[]{:S(2)}, u32[]{:S(2)}) collective-permute-start(bf16[512,512]{1,0:T(8,128)(2,1)} %collective-permute-done.5.in_a), channel_id=1, source_target_pairs={{0,2},{2,0},{4,6},{6,4},{8,10},{10,8},{12,14},{14,12},{16,18},{18,... | collective-permute-start | bytes 1572872 | tf_op jit(solution)/shard_map/ppermute | solution.py:876
  80.6 20.0 %collective-permute-start.8 = (bf16[1024,512]{1,0:T(8,128)(2,1)S(1)}, bf16[1024,512]{1,0:T(8,128)(2,1)S(1)}, u32[]{:S(2)}, u32[]{:S(2)}) collective-permute-start(bf16[1024,512]{1,0:T(8,128)(2,1)S(1)} %get-tuple-element.73), channel_id=1, source_target_pairs={{2,0},{4,2},{6,4},{8,6},{10,8},{12,10},{14,12},{16,14},{18,16},{20... | collective-permute-start | bytes 3145736 | tf_op jit(solution)/shard_map/ppermute | solution.py:930
  80.7 20.0 %collective-permute-start.9 = (bf16[1024,512]{1,0:T(8,128)(2,1)S(1)}, bf16[1024,512]{1,0:T(8,128)(2,1)S(1)}, u32[]{:S(2)}, u32[]{:S(2)}) collective-permute-start(bf16[1024,512]{1,0:T(8,128)(2,1)S(1)} %get-tuple-element.74), channel_id=1, source_target_pairs={{0,2},{2,4},{4,6},{6,8},{8,10},{10,12},{12,14},{14,16},{16,18},{18... | collective-permute-start | bytes 3145736 | tf_op jit(solution)/shard_map/ppermute | solution.py:931
  81.2 19.5 %collective-permute-start.11 = (f32[512,256]{1,0:T(8,128)S(1)}, f32[512,256]{1,0:T(8,128)S(1)}, u32[]{:S(2)}, u32[]{:S(2)}) collective-permute-start(f32[512,256]{1,0:T(8,128)S(1)} %get-tuple-element.76), channel_id=1, source_target_pairs={{0,1},{1,0},{2,3},{3,2},{4,5},{5,4},{6,7},{7,6},{8,9},{9,8},{10,11... | collective-permute-start | bytes 1572872 | tf_op jit(solution)/shard_map/ppermute | solution.py:773
  82.2 18.4 %collective-permute-start.10 = (bf16[512,256]{1,0:T(8,128)(2,1)S(1)}, bf16[512,256]{1,0:T(8,128)(2,1)S(1)}, u32[]{:S(2)}, u32[]{:S(2)}) collective-permute-start(bf16[512,256]{1,0:T(8,128)(2,1)S(1)} %get-tuple-element.75), channel_id=1, source_target_pairs={{0,1},{1,0},{2,3},{3,2},{4,5},{5,4},{6,7},{7,6},{8,9},{9,8},{10,11... | collective-permute-start | bytes 786440 | tf_op jit(solution)/shard_map/ppermute | solution.py:773
  83.2 17.4 %copy-start.15 = (f32[512]{0:T(512)S(1)}, f32[512]{0:T(512)}, u32[]{:S(2)}) copy-start(f32[512]{0:T(512)} %param.18) | copy-start | bytes 6148
  102.3 14.5 %collective-permute-start.12 = (bf16[1040,256]{1,0:T(8,128)(2,1)S(1)}, bf16[1040,256]{1,0:T(8,128)(2,1)S(1)}, u32[]{:S(2)}, u32[]{:S(2)}) collective-permute-start(bf16[1040,256]{1,0:T(8,128)(2,1)S(1)} %get-tuple-element.87), channel_id=1, source_target_pairs={{0,1},{1,0},{2,3},{3,2},{4,5},{5,4},{6,7},{7,6},{8,9},{9,8},{10,11... | collective-permute-start | bytes 1597448 | tf_op jit(solution)/shard_map/ppermute | solution.py:773
